TPU v7x, 32 devices: a whole 2x2x4 slice. The times are simulated.
32 devices in a mesh: doc: 8 (over y, x, core), vocab: 4 (over z).
Axes of the slice: x: 2, y: 2, z: 4, core: 2. Of those that a mesh axis runs over, the one named last changes fastest.
Arguments:
- tile_values: bfloat16 [8, 4, 24, 128, 128], P('doc', 'vocab'), may hold values from -6 to 6
- tile_rows: int32 [8, 4, 24], P('doc', 'vocab'), may hold values from 0 to 7, as said below
- tile_columns: int32 [8, 4, 24], P('doc', 'vocab'), may hold values from 0 to 3
- counts: int32 [8, 4], P('doc', 'vocab'), may hold values from 7 to 24, as said below
- sketch: bfloat16 [2048, 512], P('vocab'), may hold values from -6 to 6
- query_tiles: int32 [2048, 4, 4], P('doc', 'vocab'), may hold values from 0 to 3
- query_values: float32 [2048, 4, 4, 128], P('doc', 'vocab'), may hold values from -6 to 6
Outputs:
- term_basis: float32 [4, 512, 512], P('vocab', 'doc')
- projections: float32 [2048, 512], P('doc')
Inputs may be any that keep to these rules, and one draw needn't show every extreme that they name: Each device uses its first counts slots; some device uses all 24 slots in every draw. The (tile_rows, tile_columns) pairs of one device's 24 slots are all different. `query_tiles`: A query may name the same term block more than once; the values then add.
All inputs are finite; a program needn't handle non-finite values.
Results may differ from a plain program's by a relative error of at most 0.0016.
Values may be sent and summed in bfloat16 or wider, within the bound.
No kernel may reach another device: no remote copies, remote signals or barrier semaphores. Data moves between devices by JAX's collectives and lax.ppermute only.
A program may use at most 64 MiB of HBM per device.

v0:
```python
import jax
import jax.numpy as jnp
from jax import lax
from jax.sharding import PartitionSpec as P

ROW_TILES = 8
GROUP_SLOTS = 4
precise = lax.Precision.HIGHEST


def query_matrix(query_tiles, query_values, term_tiles):
    slot_tiles = query_tiles[:, 0, :]
    values = query_values[:, 0]
    onehot = (
        slot_tiles[:, :, None] == jnp.arange(term_tiles, dtype=jnp.int32)[None, None, :]
    ).astype(jnp.float32)
    placed = jnp.einsum("qtc,qti->qci", onehot, values, precision=precise)
    return placed.reshape(placed.shape[0], placed.shape[1] * placed.shape[2])


def body(tile_values, tile_rows, tile_columns, counts, sketch, query_tiles, query_values):
    blocks = tile_values[0, 0]
    row_index = tile_rows[0, 0]
    column_index = tile_columns[0, 0]
    used_slots = counts[0, 0]
    tile_edge = blocks.shape[1]
    local_terms = sketch.shape[0]
    sketch_width = sketch.shape[1]
    term_tiles = local_terms // tile_edge
    rounds = (used_slots + GROUP_SLOTS - 1) // GROUP_SLOTS
    sketch_blocks = sketch.reshape(term_tiles, tile_edge, sketch_width)
    slot_lanes = jnp.arange(GROUP_SLOTS, dtype=jnp.int32)

    def forward(step_index, totals):
        offset = step_index * GROUP_SLOTS
        group_blocks = lax.dynamic_slice_in_dim(blocks, offset, GROUP_SLOTS, 0)
        at_rows = lax.dynamic_slice_in_dim(row_index, offset, GROUP_SLOTS, 0)
        at_columns = lax.dynamic_slice_in_dim(column_index, offset, GROUP_SLOTS, 0)
        active = (offset + slot_lanes < used_slots).astype(jnp.float32)
        product = jnp.einsum(
            "sij,sjk->sik",
            group_blocks,
            sketch_blocks[at_columns],
            preferred_element_type=jnp.float32,
        )
        return totals.at[at_rows].add(product * active[:, None, None])

    start_rows = jnp.zeros((ROW_TILES, tile_edge, sketch_width), jnp.float32)
    partial_rows = lax.fori_loop(0, rounds, forward, start_rows)
    reduced = lax.psum_scatter(
        partial_rows.reshape(ROW_TILES * tile_edge, sketch_width),
        "vocab",
        scatter_dimension=0,
        tiled=True,
    )
    sketched = lax.all_gather(reduced.astype(jnp.bfloat16), "vocab", axis=0, tiled=True)
    sketched_blocks = sketched.reshape(ROW_TILES, tile_edge, sketch_width)

    def backward(step_index, totals):
        offset = step_index * GROUP_SLOTS
        group_blocks = lax.dynamic_slice_in_dim(blocks, offset, GROUP_SLOTS, 0)
        at_rows = lax.dynamic_slice_in_dim(row_index, offset, GROUP_SLOTS, 0)
        at_columns = lax.dynamic_slice_in_dim(column_index, offset, GROUP_SLOTS, 0)
        active = (offset + slot_lanes < used_slots).astype(jnp.float32)
        product = jnp.einsum(
            "sij,sik->sjk",
            group_blocks,
            sketched_blocks[at_rows],
            preferred_element_type=jnp.float32,
        )
        return totals.at[at_columns].add(product * active[:, None, None])

    start_terms = jnp.zeros((term_tiles, tile_edge, sketch_width), jnp.float32)
    term_part = lax.fori_loop(0, rounds, backward, start_terms).reshape(local_terms, sketch_width)
    query_dense = query_matrix(query_tiles, query_values, term_tiles)
    vocab_total = local_terms * lax.axis_size("vocab")
    share_rows = local_terms // lax.axis_size("doc")
    term_block = lax.psum(term_part, "doc")
    gram_part = jnp.dot(term_block.T, term_block, precision=precise)
    gram_whole = lax.psum(gram_part, "vocab")
    factor = jnp.linalg.cholesky(gram_whole / vocab_total)
    full_basis = lax.linalg.triangular_solve(
        factor, term_block, left_side=False, lower=True, transpose_a=True
    )
    basis_rows = lax.dynamic_slice_in_dim(
        full_basis, lax.axis_index("doc") * share_rows, share_rows, 0
    )
    local_projection = jnp.dot(query_dense, full_basis, precision=precise)
    projected = lax.psum(local_projection, "vocab")
    scaling = lax.rsqrt(jnp.mean(projected * projected, axis=1, keepdims=True) + 1e-06)
    return (basis_rows[None], projected * scaling)


def solution(mesh):
    return jax.shard_map(
        body,
        mesh=mesh,
        in_specs=(
            P("doc", "vocab", None, None, None),
            P("doc", "vocab", None),
            P("doc", "vocab", None),
            P("doc", "vocab"),
            P("vocab", None),
            P("doc", "vocab", None),
            P("doc", "vocab", None, None),
        ),
        out_specs=(P("vocab", "doc", None), P("doc", None)),
        check_vma=False,
    )
```

profile of v0, /device:TPU:0, one launch (start us, length us, event | category | flops | bytes accessed | tf_op | source)
XLA Modules:
  0.0 461.3 jit_solution(15977622500385682956)
XLA Ops:
  9.7 28.5 %while.24 = (s32[]{:T(128)}, f32[8,128,512]{2,1,0:T(8,128)}, s32[]{:T(128)}, s32[24]{0:T(128)S(1)}, bf16[24,128,128]{2,1,0:T(8,128)(2,1)S(1)}, /*index=5*/s32[24...) while((s32[]{:T(128)}, f32[8,128,512]{2,1,0:T(8,128)}, ...), condition=%wide.region_2.3_spmd.clone, body=%wide.region_0.2_spmd.clone.sunk | while | flops 67634216 | bytes 5903155 | solution.py:49
  11.3 3.2 scatter_fusion
  16.1 3.1 scatter_fusion
  20.9 3.2 scatter_fusion
  25.7 3.2 scatter_fusion
  30.4 3.1 scatter_fusion
  35.2 3.0 scatter_fusion
  38.3 46.3 %reduce-scatter.2.cloned.1.call-done = f32[256,512]{1,0:T(8,128)} async-done(((f32[1024,512]{1,0:T(8,128)}), f32[256,512]{1,0:T(8,128)}) %reduce-scatter.2.cloned.1.call-update) | async-done | bytes 524304 | tf_op jit(solution)/shard_map/reduce_scatter | solution.py:50
  87.6 26.3 %all-gather.2.cloned.1.call-done = bf16[1024,512]{1,0:T(8,128)(2,1)} async-done(((bf16[256,512]{1,0:T(8,128)(2,1)}), bf16[1024,512]{1,0:T(8,128)(2,1)}) %all-gather.2.cloned.1.call-update) | async-done | bytes 1048592 | tf_op jit(solution)/shard_map/all_gather | solution.py:56
  114.1 29.6 %while.25 = (s32[]{:T(128)}, f32[4,128,512]{2,1,0:T(8,128)S(1)}, s32[]{:T(128)}, s32[24]{0:T(128)S(1)}, bf16[24,128,128]{1,2,0:T(8,128)(2,1)}, /*index=5*/s32[24...) while((s32[]{:T(128)}, f32[4,128,512]{2,1,0:T(8,128)S(1)}, ...), condition=%wide.region_6.7_spmd.clone, body=%wide.region_4.6_spmd.clone.sunk | while | flops 67634216 | bytes 5902659 | solution.py:74
  144.8 56.1 %all-reduce.5.cloned.1.call-done = f32[512,512]{1,0:T(8,128)} async-done(((f32[512,512]{1,0:T(8,128)}), f32[512,512]{1,0:T(8,128)}) %all-reduce.5.cloned.1.call-update) | async-done | bytes 1048592 | tf_op jit(solution)/shard_map/psum | solution.py:78
  201.0 4.4 fusion.45
  207.1 49.6 %all-reduce.7.cloned.1.call-done = f32[512,512]{0,1:T(8,128)} async-done(((f32[512,512]{0,1:T(8,128)}), f32[512,512]{0,1:T(8,128)}) %all-reduce.7.cloned.1.call-update) | async-done | bytes 1048592 | tf_op jit(solution)/shard_map/psum | solution.py:80
  261.9 11.7 %cholesky.104 = f32[128,128]{1,0:T(8,128)S(1)} custom-call(f32[128,128]{1,0:T(8,128)S(1)} %cholesky.266), custom_call_target="Cholesky" | custom-call | tf_op jit(solution)/shard_map/jit(cholesky)/cholesky | solution.py:81
  273.8 9.8 %custom-call.30 = f32[1,128,128]{1,2,0:T(8,128)S(1)} custom-call(f32[1,128,128]{2,1,0:T(8,128)S(1)} %get-tuple-element.217), custom_call_target="InvertDiagBlocksLowerTriangular" | custom-call | tf_op jit(solution)/shard_map/jit(cholesky)/cholesky | solution.py:81
  286.2 11.8 %cholesky.217 = f32[128,128]{1,0:T(8,128)S(1)} custom-call(f32[128,128]{1,0:T(8,128)S(1)} %cholesky.270), custom_call_target="Cholesky" | custom-call | tf_op jit(solution)/shard_map/jit(cholesky)/cholesky | solution.py:81
  298.0 9.8 %custom-call.31 = f32[1,128,128]{1,2,0:T(8,128)S(1)} custom-call(f32[1,128,128]{2,1,0:T(8,128)S(1)} %get-tuple-element.214), custom_call_target="InvertDiagBlocksLowerTriangular" | custom-call | tf_op jit(solution)/shard_map/jit(cholesky)/cholesky | solution.py:81
  309.4 11.7 %cholesky.238 = f32[128,128]{1,0:T(8,128)S(1)} custom-call(f32[128,128]{1,0:T(8,128)S(1)} %cholesky.275), custom_call_target="Cholesky" | custom-call | tf_op jit(solution)/shard_map/jit(cholesky)/cholesky | solution.py:81
  321.8 9.8 %custom-call.32 = f32[1,128,128]{1,2,0:T(8,128)S(1)} custom-call(f32[1,128,128]{2,1,0:T(8,128)S(1)} %get-tuple-element.211), custom_call_target="InvertDiagBlocksLowerTriangular" | custom-call | tf_op jit(solution)/shard_map/jit(cholesky)/cholesky | solution.py:81
  333.1 11.9 %cholesky.255 = f32[128,128]{1,0:T(8,128)S(1)} custom-call(f32[128,128]{1,0:T(8,128)S(1)} %convolution_subtract_fusion.5), custom_call_target="Cholesky" | custom-call | tf_op jit(solution)/shard_map/jit(cholesky)/cholesky | solution.py:81
  350.1 13.8 %while.23 = (s32[]{:T(128)}, f32[512,512]{1,0:T(8,128)}, s32[4,2]{0,1:T(2,128)S(1)}, f32[4,128,128]{2,1,0:T(8,128)}, s32[]{:T(128)}) while((s32[]{:T(128)}, f32[512,512]{1,0:T(8,128)}, s32[4,2]{0,1:T(2,128)S(1)}, f32[4,128,128]{2,1,0:T(8,128)}, s32[]{:T(128)}) %tuple.77), condition=%wide.while_cond, body=%wide.while_body.sunk | while | flops 2 | bytes 132705 | solution.py:82
  350.7 2.9 bitcast_dynamic-update-slice_fusion.2
  363.9 40.1 %custom-call.33 = f32[4,128,128]{1,2,0:T(8,128)S(1)} custom-call(f32[4,128,128]{2,1,0:T(8,128)} %get-tuple-element.107), custom_call_target="InvertDiagBlocksLowerTriangular" | custom-call | tf_op jit(solution)/shard_map/triangular_solve | solution.py:82
  414.4 37.1 %all-reduce.9.cloned.1.call-done = f32[256,512]{1,0:T(8,128)} async-done(((f32[256,512]{1,0:T(8,128)}), f32[256,512]{1,0:T(8,128)}) %all-reduce.9.cloned.1.call-update) | async-done | bytes 524304 | tf_op jit(solution)/shard_map/psum | solution.py:89
  (151 shorter events, 85.0 us)
Async XLA Ops:
  7.2 198.9 %copy-start = (f32[256,1,4,128]{3,2,1,0:T(4,128)S(1)}, f32[256,1,4,128]{3,2,1,0:T(4,128)}, u32[]{:S(2)}) copy-start(f32[256,1,4,128]{3,2,1,0:T(4,128)} %param.17) | copy-start | bytes 1572868
  7.2 2.5 copy-start.8
  7.2 2.5 copy-start.7
  7.2 2.5 copy-start.6
  7.2 2.5 copy-start.2
  7.2 77.4 %reduce-scatter.2.cloned.1.call-start = ((), (), s32[]{:S(2)}) async-start(), calls=%async_computation.1 | async-start | bytes 2621440 | tf_op jit(solution)/shard_map/reduce_scatter | solution.py:50
  38.2 75.7 %all-gather.2.cloned.1.call-start = ((), (), s32[]{:S(2)}) async-start(), calls=%async_computation.2 | async-start | bytes 1310720 | tf_op jit(solution)/shard_map/all_gather | solution.py:56
  86.4 114.6 %all-reduce.5.cloned.1.call-start = ((), (), s32[]{:S(2)}) async-start(), calls=%async_computation.3 | async-start | bytes 2097152 | tf_op jit(solution)/shard_map/psum | solution.py:78
  143.7 1.0 copy-start.1
  144.8 61.2 %copy-start.9 = (s32[256,1,4]{0,2,1:T(4,128)S(1)}, s32[256,1,4]{0,2,1:T(4,128)}, u32[]{:S(2)}) copy-start(s32[256,1,4]{0,2,1:T(4,128)} %param.16) | copy-start | bytes 12292
  144.8 111.9 %all-reduce.7.cloned.1.call-start = ((), (), s32[]{:S(2)}) async-start(), calls=%async_computation.4 | async-start | bytes 2097152 | tf_op jit(solution)/shard_map/psum | solution.py:80
  205.4 246.0 %all-reduce.9.cloned.1.call-start = ((), (), s32[]{:S(2)}) async-start(), calls=%async_computation.5 | async-start | bytes 1048576 | tf_op jit(solution)/shard_map/psum | solution.py:89
  256.7 4.0 copy-start.4
  260.9 1.0 copy-start.5
  309.4 94.7 %copy-start.3 = (f32[512,512]{1,0:T(8,128)S(1)}, f32[512,512]{1,0:T(8,128)}, u32[]{:S(2)}) copy-start(f32[512,512]{1,0:T(8,128)} %all-reduce.5.cloned.1.call-done) | copy-start | bytes 3145732
Sparse Core Ops, SparseCore 0:
  38.4 46.1 reduce-scatter.1
  86.7 27.1 all-gather.1
  144.9 56.0 all-reduce.4
  205.5 51.1 all-reduce.6
  413.5 37.9 all-reduce.8
where the time goes:
time: 466 us; the launch traced here: 461 us
  waiting for transfers between devices  215 us (46%)
  other arithmetic  162 us (35%)
  local copies, waits for them, and re-layouts  35.9 us (8%)
  matrix products  28.9 us (6%)
  between operations  17.7 us (4%)
    another operation x14, other arithmetic, body(): factor = jnp.linalg.cholesky(gram_whole / vocab_total)  78.8 us
    psum x1, waiting for transfers between devices, body(): term_block = lax.psum(term_part, 'doc')  56.1 us
    psum x1, waiting for transfers between devices, body(): gram_whole = lax.psum(gram_part, 'vocab')  49.6 us
    reduce_scatter x1, waiting for transfers between devices, body(): lax.psum_scatter(partial_rows.reshape(ROW_TILES * tile_edge, sketch_width...  46.3 us
    another operation x4, other arithmetic, body(): lax.linalg.triangular_solve(factor, term_block, left_side=False, lower=Tr...  41.4 us
    psum x1, waiting for transfers between devices, body(): projected = lax.psum(local_projection, 'vocab')  37.1 us
    all_gather x1, waiting for transfers between devices, body(): lax.all_gather(reduced.astype(jnp.bfloat16), 'vocab', axis=0, tiled=True)  26.3 us
    scatter-add x6, other arithmetic, forward(): return totals.at[at_rows].add(product * active[:, None, None])  18.8 us
  transfers between devices with their start and end apart: 5, of which 5 were waited for; matrix products, arithmetic and copies ran while one was open for 1% of the time, Pallas kernels for 0%

commit v1 on v0

--- a/solution.py
+++ b/solution.py
@@ -53,7 +53,12 @@
         scatter_dimension=0,
         tiled=True,
     )
-    sketched = lax.all_gather(reduced.astype(jnp.bfloat16), "vocab", axis=0, tiled=True)
+    sketched = jnp.concatenate(
+        lax.all_to_all(
+            jnp.stack([reduced.astype(jnp.bfloat16)] * lax.axis_size("vocab")), "vocab", 0, 0
+        ),
+        axis=0,
+    )
     sketched_blocks = sketched.reshape(ROW_TILES, tile_edge, sketch_width)
 
     def backward(step_index, totals):

time: 466 us -> 469 us (level)
    all_gather x1 -> x0, waiting for transfers between devices: 26.3 us -> none  [body(): lax.all_gather(reduced.astype(jnp.bfloat16), 'vocab', axis=0, tiled=True)]
    all_to_all x0 -> x1, waiting for transfers between devices: none -> 24.4 us  [body(): lax.all_to_all(jnp.stack([reduced.astype(jnp.bfloat16)] * lax.axis_size('...]
    another operation x12 -> x13, local copies, waits for them, and re-layouts: 13.8 us -> 14.9 us
where the time goes in v1:
time: 469 us; the launch traced here: 464 us
  waiting for transfers between devices  213 us (45%)
  other arithmetic  161 us (34%)
  local copies, waits for them, and re-layouts  37 us (8%)
  matrix products  28.9 us (6%)
  between operations  17.7 us (4%)
  starting transfers between devices  4.86 us (1%)
    another operation x14, other arithmetic, body(): factor = jnp.linalg.cholesky(gram_whole / vocab_total)  78.8 us
    psum x1, waiting for transfers between devices, body(): term_block = lax.psum(term_part, 'doc')  55.8 us
    psum x1, waiting for transfers between devices, body(): gram_whole = lax.psum(gram_part, 'vocab')  49.6 us
    reduce_scatter x1, waiting for transfers between devices, body(): lax.psum_scatter(partial_rows.reshape(ROW_TILES * tile_edge, sketch_width...  46.3 us
    another operation x4, other arithmetic, body(): lax.linalg.triangular_solve(factor, term_block, left_side=False, lower=Tr...  41.4 us
    psum x1, waiting for transfers between devices, body(): projected = lax.psum(local_projection, 'vocab')  36.9 us
    all_to_all x1, waiting for transfers between devices, body(): lax.all_to_all(jnp.stack([reduced.astype(jnp.bfloat16)] * lax.axis_size('...  24.4 us
    scatter-add x6, other arithmetic, forward(): return totals.at[at_rows].add(product * active[:, None, None])  18.8 us
  transfers between devices with their start and end apart: 5, of which 5 were waited for; matrix products, arithmetic and copies ran while one was open for 1% of the time, Pallas kernels for 0%

profile of v1, /device:TPU:0, one launch (start us, length us, event | category | flops | bytes accessed | tf_op | source)
XLA Modules:
  0.0 463.6 jit_solution(1966326896568137801)
XLA Ops:
  9.7 28.5 %while.24 = (s32[]{:T(128)}, f32[8,128,512]{2,1,0:T(8,128)}, s32[]{:T(128)}, s32[24]{0:T(128)S(1)}, bf16[24,128,128]{2,1,0:T(8,128)(2,1)S(1)}, /*index=5*/s32[24...) while((s32[]{:T(128)}, f32[8,128,512]{2,1,0:T(8,128)}, ...), condition=%wide.region_2.3_spmd.clone, body=%wide.region_0.2_spmd.clone.sunk | while | flops 67634216 | bytes 5903155 | solution.py:49
  11.3 3.2 scatter_fusion
  16.1 3.1 scatter_fusion
  20.9 3.2 scatter_fusion
  25.7 3.2 scatter_fusion
  30.4 3.1 scatter_fusion
  35.2 3.0 scatter_fusion
  38.2 46.3 %reduce-scatter.2.cloned.1.call-done = f32[256,512]{1,0:T(8,128)} async-done(((f32[1024,512]{1,0:T(8,128)}), f32[256,512]{1,0:T(8,128)}) %reduce-scatter.2.cloned.1.call-update) | async-done | bytes 524304 | tf_op jit(solution)/shard_map/reduce_scatter | solution.py:50
  86.8 4.2 all-to-all-start
  92.3 24.4 %all-to-all-done = bf16[4,256,512]{2,1,0:T(8,128)(2,1)} async-done(((bf16[4,256,512]{2,1,0:T(8,128)(2,1)}), bf16[4,256,512]{2,1,0:T(8,128)(2,1)}, u32[]{:S(2)}, u32[]{:S(2)}) %all-to-all-start) | async-done | bytes 1048608 | tf_op jit(solution)/shard_map/all_to_all | solution.py:57
  116.8 29.6 %while.25 = (s32[]{:T(128)}, f32[4,128,512]{2,1,0:T(8,128)S(1)}, s32[]{:T(128)}, s32[24]{0:T(128)S(1)}, bf16[24,128,128]{1,2,0:T(8,128)(2,1)}, /*index=5*/s32[24...) while((s32[]{:T(128)}, f32[4,128,512]{2,1,0:T(8,128)S(1)}, ...), condition=%wide.region_6.7_spmd.clone, body=%wide.region_4.6_spmd.clone.sunk | while | flops 67634216 | bytes 5902659 | solution.py:79
  147.6 55.8 %all-reduce.5.cloned.1.call-done = f32[512,512]{1,0:T(8,128)} async-done(((f32[512,512]{1,0:T(8,128)}), f32[512,512]{1,0:T(8,128)}) %all-reduce.5.cloned.1.call-update) | async-done | bytes 1048592 | tf_op jit(solution)/shard_map/psum | solution.py:83
  203.4 4.4 fusion.45
  209.5 49.6 %all-reduce.7.cloned.1.call-done = f32[512,512]{0,1:T(8,128)} async-done(((f32[512,512]{0,1:T(8,128)}), f32[512,512]{0,1:T(8,128)}) %all-reduce.7.cloned.1.call-update) | async-done | bytes 1048592 | tf_op jit(solution)/shard_map/psum | solution.py:85
  264.3 11.7 %cholesky.104 = f32[128,128]{1,0:T(8,128)S(1)} custom-call(f32[128,128]{1,0:T(8,128)S(1)} %cholesky.266), custom_call_target="Cholesky" | custom-call | tf_op jit(solution)/shard_map/jit(cholesky)/cholesky | solution.py:86
  276.2 9.8 %custom-call.30 = f32[1,128,128]{1,2,0:T(8,128)S(1)} custom-call(f32[1,128,128]{2,1,0:T(8,128)S(1)} %get-tuple-element.217), custom_call_target="InvertDiagBlocksLowerTriangular" | custom-call | tf_op jit(solution)/shard_map/jit(cholesky)/cholesky | solution.py:86
  288.6 11.8 %cholesky.217 = f32[128,128]{1,0:T(8,128)S(1)} custom-call(f32[128,128]{1,0:T(8,128)S(1)} %cholesky.270), custom_call_target="Cholesky" | custom-call | tf_op jit(solution)/shard_map/jit(cholesky)/cholesky | solution.py:86
  300.4 9.8 %custom-call.31 = f32[1,128,128]{1,2,0:T(8,128)S(1)} custom-call(f32[1,128,128]{2,1,0:T(8,128)S(1)} %get-tuple-element.214), custom_call_target="InvertDiagBlocksLowerTriangular" | custom-call | tf_op jit(solution)/shard_map/jit(cholesky)/cholesky | solution.py:86
  311.8 11.7 %cholesky.238 = f32[128,128]{1,0:T(8,128)S(1)} custom-call(f32[128,128]{1,0:T(8,128)S(1)} %cholesky.275), custom_call_target="Cholesky" | custom-call | tf_op jit(solution)/shard_map/jit(cholesky)/cholesky | solution.py:86
  324.2 9.8 %custom-call.32 = f32[1,128,128]{1,2,0:T(8,128)S(1)} custom-call(f32[1,128,128]{2,1,0:T(8,128)S(1)} %get-tuple-element.211), custom_call_target="InvertDiagBlocksLowerTriangular" | custom-call | tf_op jit(solution)/shard_map/jit(cholesky)/cholesky | solution.py:86
  335.5 11.9 %cholesky.255 = f32[128,128]{1,0:T(8,128)S(1)} custom-call(f32[128,128]{1,0:T(8,128)S(1)} %convolution_subtract_fusion.5), custom_call_target="Cholesky" | custom-call | tf_op jit(solution)/shard_map/jit(cholesky)/cholesky | solution.py:86
  352.5 13.8 %while.23 = (s32[]{:T(128)}, f32[512,512]{1,0:T(8,128)}, s32[4,2]{0,1:T(2,128)S(1)}, f32[4,128,128]{2,1,0:T(8,128)}, s32[]{:T(128)}) while((s32[]{:T(128)}, f32[512,512]{1,0:T(8,128)}, s32[4,2]{0,1:T(2,128)S(1)}, f32[4,128,128]{2,1,0:T(8,128)}, s32[]{:T(128)}) %tuple.77), condition=%wide.while_cond, body=%wide.while_body.sunk | while | flops 2 | bytes 132705 | solution.py:87
  366.3 40.1 %custom-call.33 = f32[4,128,128]{1,2,0:T(8,128)S(1)} custom-call(f32[4,128,128]{2,1,0:T(8,128)} %get-tuple-element.107), custom_call_target="InvertDiagBlocksLowerTriangular" | custom-call | tf_op jit(solution)/shard_map/triangular_solve | solution.py:87
  416.8 36.9 %all-reduce.9.cloned.1.call-done = f32[256,512]{1,0:T(8,128)} async-done(((f32[256,512]{1,0:T(8,128)}), f32[256,512]{1,0:T(8,128)}) %all-reduce.9.cloned.1.call-update) | async-done | bytes 524304 | tf_op jit(solution)/shard_map/psum | solution.py:94
  (151 shorter events, 88.2 us)
Async XLA Ops:
  7.2 201.3 %copy-start = (f32[256,1,4,128]{3,2,1,0:T(4,128)S(1)}, f32[256,1,4,128]{3,2,1,0:T(4,128)}, u32[]{:S(2)}) copy-start(f32[256,1,4,128]{3,2,1,0:T(4,128)} %param.17) | copy-start | bytes 1572868
  7.2 2.5 copy-start.8
  7.2 2.5 copy-start.7
  7.2 2.5 copy-start.6
  7.2 2.5 copy-start.2
  7.2 77.4 %reduce-scatter.2.cloned.1.call-start = ((), (), s32[]{:S(2)}) async-start(), calls=%async_computation.2 | async-start | bytes 2621440 | tf_op jit(solution)/shard_map/reduce_scatter | solution.py:50
  86.8 29.9 %all-to-all-start = ((bf16[4,256,512]{2,1,0:T(8,128)(2,1)}), bf16[4,256,512]{2,1,0:T(8,128)(2,1)}, u32[]{:S(2)}, u32[]{:S(2)}) async-start(bf16[4,256,512]{2,1,0:T(8,128)(2,1)} %stack.2), calls=%async_computation.1 | async-start | bytes 2097152 | tf_op jit(solution)/shard_map/all_to_all | solution.py:57
  91.0 112.4 %all-reduce.5.cloned.1.call-start = ((), (), s32[]{:S(2)}) async-start(), calls=%async_computation.3 | async-start | bytes 2097152 | tf_op jit(solution)/shard_map/psum | solution.py:83
  146.4 1.0 copy-start.1
  147.5 60.8 %copy-start.9 = (s32[256,1,4]{0,2,1:T(4,128)S(1)}, s32[256,1,4]{0,2,1:T(4,128)}, u32[]{:S(2)}) copy-start(s32[256,1,4]{0,2,1:T(4,128)} %param.16) | copy-start | bytes 12292
  147.5 111.6 %all-reduce.7.cloned.1.call-start = ((), (), s32[]{:S(2)}) async-start(), calls=%async_computation.4 | async-start | bytes 2097152 | tf_op jit(solution)/shard_map/psum | solution.py:85
  207.8 245.9 %all-reduce.9.cloned.1.call-start = ((), (), s32[]{:S(2)}) async-start(), calls=%async_computation.5 | async-start | bytes 1048576 | tf_op jit(solution)/shard_map/psum | solution.py:94
  259.1 4.0 copy-start.4
  263.3 1.0 copy-start.5
  311.8 94.6 %copy-start.3 = (f32[512,512]{1,0:T(8,128)S(1)}, f32[512,512]{1,0:T(8,128)}, u32[]{:S(2)}) copy-start(f32[512,512]{1,0:T(8,128)} %all-reduce.5.cloned.1.call-done) | copy-start | bytes 3145732
Sparse Core Ops, SparseCore 0:
  38.4 46.1 reduce-scatter.1
  147.6 55.7 all-reduce.4
  207.9 51.1 all-reduce.6
  415.9 37.7 all-reduce.8
